TPU v7x, 256 devices: a whole 4x4x8 slice. The times are simulated.
256 devices in a mesh: group: 32 (over z, x_lo, core), rep: 8 (over x_hi, y).
Axes of the slice: x: 4 (x_hi: 2, x_lo: 2; x = x_hi * 2 + x_lo), y: 4, z: 8, core: 2. Of those that a mesh axis runs over, the one named last changes fastest.
Arguments:
- queries: bfloat16 [256, 256, 3072], P(('group', 'rep')), may hold values from -46 to 46
- keys: bfloat16 [256, 256, 3072], P(('group', 'rep')), may hold values from -46 to 46
- values: bfloat16 [256, 256, 3072], P(('group', 'rep')), may hold values from -24 to 24
- grad_output: bfloat16 [256, 256, 3072], P(('group', 'rep')), may hold values from -6 to 6
- weight_codes: bfloat16 [3072, 3072], P('group'), may hold values from -4 to 4
- weight_scales: float32 [3072, 12], P('group'), may hold values from 0.006 to 0.06
Outputs:
- grad_queries: bfloat16 [256, 256, 3072], P(('group', 'rep'))
- grad_keys: bfloat16 [256, 256, 3072], P(('group', 'rep'))
- grad_values: bfloat16 [256, 256, 3072], P(('group', 'rep'))
- grad_weight: float32 [3072, 3072], P(('group', 'rep'))
All inputs are finite; a program needn't handle non-finite values.
Results may differ from a plain program's by a relative error of at most 0.029.
Values may be sent and summed in bfloat16 or wider, within the bound.
No kernel may reach another device: no remote copies, remote signals or barrier semaphores. Data moves between devices by JAX's collectives and lax.ppermute only.
A program may use at most 128 MiB of HBM per device.

v0:
```python
import jax
import jax.numpy as jnp
from jax import lax
from jax.sharding import Mesh
from jax.sharding import PartitionSpec as P

HD = 128
GROUP = ("group_0", "group_1", "group_2")
GROUP_REP = ("group_0", "group_1", "group_2", "rep")


def from_everyone(value, axis):
    count = lax.axis_size(axis)
    return lax.all_to_all(
        jnp.broadcast_to(value[None], (count, *value.shape)), axis, 0, 0, tiled=True
    )


def in_order(pieces, dim):
    shape = list(pieces.shape[1:])
    shape[dim] *= pieces.shape[0]
    return jnp.moveaxis(pieces, 0, dim).reshape(shape)


def gather_axes(value, axes, dim):
    far, near = axes
    pieces = from_everyone(from_everyone(value, far), near)
    return in_order(pieces.swapaxes(0, 1).reshape(-1, *value.shape), dim)


def cut_along(value, dim, count):
    before, after = (value.shape[:dim], value.shape[dim + 1 :])
    return jnp.moveaxis(value.reshape(*before, count, -1, *after), dim, 0)


def sent_and_summed(value, axis, dim):
    count = lax.axis_size(axis)
    pieces = lax.all_to_all(cut_along(value, dim, count), axis, 0, 0, tiled=True)
    return jnp.sum(pieces, axis=0)


def sum_in_two_steps(value, axes, dim):
    far, near = axes
    pieces = cut_along(value, dim, lax.axis_size(far))
    nearer = sent_and_summed(pieces, near, dim + 1)
    arrived = lax.all_to_all(nearer, far, split_axis=0, concat_axis=0, tiled=True)
    return arrived.sum(axis=0)


def restore(code_rows, scale_rows):
    row_count = code_rows.shape[0]
    block_count = scale_rows.shape[1]
    spread = (
        code_rows.astype(jnp.float32).reshape(row_count, block_count, -1) * scale_rows[:, :, None]
    )
    return spread.reshape(row_count, -1).astype(jnp.bfloat16)


def forward_image(arrays_in):
    query, keyset, valueset = arrays_in
    seq_len = query.shape[0]
    head_count = query.shape[1] // HD
    query_heads = query.reshape(seq_len, head_count, HD)
    key_heads = keyset.reshape(seq_len, head_count, HD)
    value_heads = valueset.reshape(seq_len, head_count, HD)
    scores = jnp.einsum(
        "qhd,khd->hqk", query_heads, key_heads, preferred_element_type=jnp.float32
    ) * HD ** (-0.5)
    highest = jnp.max(scores, axis=2, keepdims=True)
    exponent = jnp.exp(scores - highest)
    probability = exponent / jnp.sum(exponent, axis=2, keepdims=True)
    weight_half = probability.astype(jnp.bfloat16)
    context = jnp.einsum(
        "hqk,khd->qhd", weight_half, value_heads, preferred_element_type=jnp.float32
    )
    return (probability, context.astype(jnp.bfloat16).reshape(seq_len, -1))


def backward_image(arrays_in):
    query, keyset, valueset, probability, grad_context = arrays_in
    seq_len = query.shape[0]
    head_count = query.shape[1] // HD
    query_heads = query.reshape(seq_len, head_count, HD)
    key_heads = keyset.reshape(seq_len, head_count, HD)
    value_heads = valueset.reshape(seq_len, head_count, HD)
    grad_heads = grad_context.reshape(seq_len, head_count, HD)
    weight_half = probability.astype(jnp.bfloat16)
    grad_value = jnp.einsum(
        "hqk,qhd->khd", weight_half, grad_heads, preferred_element_type=jnp.float32
    )
    dprobs = jnp.einsum("qhd,khd->hqk", grad_heads, value_heads, preferred_element_type=jnp.float32)
    row_delta = jnp.sum(probability * dprobs, axis=2, keepdims=True)
    dscores = (probability * (dprobs - row_delta) * HD ** (-0.5)).astype(jnp.bfloat16)
    grad_query = jnp.einsum("hqk,khd->qhd", dscores, key_heads, preferred_element_type=jnp.float32)
    grad_key = jnp.einsum("hqk,qhd->khd", dscores, query_heads, preferred_element_type=jnp.float32)
    return (
        grad_query.astype(jnp.bfloat16).reshape(seq_len, -1),
        grad_key.astype(jnp.bfloat16).reshape(seq_len, -1),
        grad_value.astype(jnp.bfloat16).reshape(seq_len, -1),
    )


def per_device(queries, keys, values, grad_output, weight_codes, weight_scales):
    image_count, seq_len, row_total = queries.shape
    feature_count = grad_output.shape[2]
    local_rows = image_count * seq_len
    probability, contexts = lax.map(forward_image, (queries, keys, values))
    context_flat = contexts.reshape(local_rows, row_total)
    output_flat = grad_output.reshape(local_rows, feature_count)
    group_count = lax.axis_size(GROUP)
    replica_count = lax.axis_size("rep")
    slab_rows = row_total // (group_count * replica_count)
    first_row = lax.axis_index("rep") * slab_rows
    codes_part = lax.dynamic_slice_in_dim(weight_codes, first_row, slab_rows, 0)
    scales_part = lax.dynamic_slice_in_dim(weight_scales, first_row, slab_rows, 0)
    all_output = lax.all_gather(output_flat, "rep", axis=0, tiled=True)
    split_context = jnp.moveaxis(
        context_flat.reshape(local_rows, group_count, replica_count, slab_rows), 2, 0
    )
    split_context = split_context.reshape(replica_count, local_rows, group_count * slab_rows)
    gathered_ctx = lax.all_to_all(split_context, "rep", split_axis=0, concat_axis=1, tiled=True)
    gathered_ctx = gathered_ctx.reshape(replica_count, local_rows, group_count * slab_rows)
    grad_columns = jnp.dot(
        all_output,
        restore(
            gather_axes(codes_part, (("group_0", "group_1"), "group_2"), 0),
            gather_axes(
                scales_part.astype(jnp.bfloat16), (("group_0", "group_1"), "group_2"), 0
            ).astype(scales_part.dtype),
        ).T,
        preferred_element_type=jnp.float32,
    ).astype(jnp.bfloat16)
    output_blocks = all_output.reshape(replica_count, local_rows, feature_count)
    device_terms = jnp.einsum(
        "rlp,rle->rpe", gathered_ctx, output_blocks, preferred_element_type=jnp.float32
    ).astype(jnp.bfloat16)
    grad_weight = sum_in_two_steps(
        jnp.sum(lax.optimization_barrier(device_terms).astype(jnp.float32), axis=0),
        (("group_0", "group_1"), "group_2"),
        0,
    )
    returned = lax.all_to_all(
        grad_columns.reshape(1, replica_count * local_rows, group_count * slab_rows),
        "rep",
        split_axis=1,
        concat_axis=0,
        tiled=True,
    )
    returned = jnp.moveaxis(
        returned.reshape(replica_count, local_rows, group_count, slab_rows), 0, 2
    )
    grad_context = returned.reshape(image_count, seq_len, row_total)
    grad_queries, grad_keys, grad_values = lax.map(
        backward_image, (queries, keys, values, probability, grad_context)
    )
    return (grad_queries, grad_keys, grad_values, grad_weight)


def solution(mesh):
    split = Mesh(
        mesh.devices.reshape(8, 2, 2, mesh.shape["rep"]), ("group_0", "group_1", "group_2", "rep")
    )
    return jax.shard_map(
        per_device,
        mesh=split,
        in_specs=(
            P(GROUP_REP, None, None),
            P(GROUP_REP, None, None),
            P(GROUP_REP, None, None),
            P(GROUP_REP, None, None),
            P(GROUP, None),
            P(GROUP, None),
        ),
        out_specs=(
            P(GROUP_REP, None, None),
            P(GROUP_REP, None, None),
            P(GROUP_REP, None, None),
            P(GROUP_REP, None),
        ),
        check_vma=False,
    )
```

profile of v0, /device:TPU:4, one launch (start us, length us, event | category | flops | bytes accessed | tf_op | source)
XLA Modules:
  0.0 398.7 jit_solution(12941961424991909647)
XLA Ops:
  7.2 0.0 copy-start
  7.2 0.0 all-gather.3.cloned.1.call-start
  7.2 0.7 all-gather.3.cloned.1.call-update
  7.9 0.9 dynamic-slice_convert_fusion
  8.8 0.6 broadcast_in_dim.52
  9.5 9.2 %all-to-all-start.2 = ((bf16[16,12,12]{1,2,0:T(8,128)(2,1)}), bf16[16,12,12]{1,2,0:T(8,128)(2,1)S(1)}, u32[]{:S(2)}, u32[]{:S(2)}) async-start(bf16[16,12,12]{1,2,0:T(8,128)(2,1)} %broadcast_in_dim.52), calls=%async_computation.2 | async-start | bytes 131072 | tf_op jit(solution)/shard_map/all_to_all | solution.py:14
  18.7 9.0 %all-to-all-done.2 = bf16[16,12,12]{1,2,0:T(8,128)(2,1)S(1)} async-done(((bf16[16,12,12]{1,2,0:T(8,128)(2,1)}), bf16[16,12,12]{1,2,0:T(8,128)(2,1)S(1)}, u32[]{:S(2)}, u32[]{:S(2)}) %all-to-all-start.2) | async-done | bytes 4640 | tf_op jit(solution)/shard_map/all_to_all | solution.py:14
  27.8 0.2 reshape.109
  27.9 3.7 all_to_all.48
  31.6 1.3 broadcast_in_dim.50
  33.0 4.4 %all-to-all-start = ((bf16[16,12,3072]{2,1,0:T(8,128)(2,1)}), bf16[16,12,3072]{2,1,0:T(8,128)(2,1)}, u32[]{:S(2)}, u32[]{:S(2)}) async-start(bf16[16,12,3072]{2,1,0:T(8,128)(2,1)} %broadcast_in_dim.50), calls=%async_computation | async-start | bytes 3145728 | tf_op jit(solution)/shard_map/all_to_all | solution.py:14
  37.4 1.6 copy.148
  39.0 2.6 copy.147
  41.6 1.7 copy.149
  43.3 0.0 copy-start.3
  43.3 7.4 %fusion.43 = (f32[24,256]{1,0:T(8,128)S(1)}, f32[24,256,256]{1,2,0:T(8,128)}) fusion(bf16[256,24,128]{0,2,1:T(8,128)(2,1)} %bitcast.77, bf16[256,24,128]{0,2,1:T(8,128)(2,1)} %bitcast.79), kind=kOutput, calls=%fused_computation.38 | convolution fusion | flops 407372032 | bytes 9461760 | tf_op jit(solution)/shard_map/while/body/eval_jaxpr/sub | solution.py:70
  50.7 4.6 %fusion.33 = bf16[256,24,128]{0,2,1:T(8,128)(2,1)} fusion(bf16[256,24,128]{0,2,1:T(8,128)(2,1)S(1)} %bitcast.72, f32[24,256,256]{1,2,0:T(8,128)} %get-tuple-element.74, f32[24,256]{1,0:T(8,128)S(1)} %get-tuple-element.73), kind=kOutput, calls=%fused_computation.28 | convolution fusion | flops 406585344 | bytes 9461760 | tf_op jit(solution)/shard_map/while/body/eval_jaxpr/hqk,khd->qhd/dot_general | solution.py:73
  55.3 2.4 reshape_reshape.8
  57.6 0.7 copy.135
  58.4 1.5 copy.136
  59.8 0.2 reshape.110
  60.1 0.2 copy.121
  60.2 0.3 reshape.106
  60.5 2.4 mul.32
  63.0 6.1 %copy.122 = f32[384,3072]{1,0:T(8,128)} copy(f32[384,3072]{0,1:T(8,128)} %bitcast.67) | data formatting | bytes 9437184 | tf_op jit(solution)/shard_map/mul | solution.py:54
  69.0 8.3 %all-to-all-done = bf16[16,12,3072]{2,1,0:T(8,128)(2,1)} async-done(((bf16[16,12,3072]{2,1,0:T(8,128)(2,1)}), bf16[16,12,3072]{2,1,0:T(8,128)(2,1)}, u32[]{:S(2)}, u32[]{:S(2)}) %all-to-all-start) | async-done | bytes 1179680 | tf_op jit(solution)/shard_map/all_to_all | solution.py:14
  77.3 2.1 copy.118
  79.4 0.3 broadcast_in_dim.51
  79.7 5.6 %all_to_all.49 = bf16[2,16,12,3072]{3,1,2,0:T(8,128)(2,1)S(1)} all-to-all(bf16[2,16,12,3072]{3,1,2,0:T(8,128)(2,1)S(1)} %broadcast_in_dim.51), channel_id=1, replica_groups=mesh['group_0'=8,'group_1'=2,'group_2'=2,'rep'=8] {'group_2'}, dimensions={0} | all-to-all | bytes 4718592 | tf_op jit(solution)/shard_map/all_to_all | solution.py:14
  85.3 8.0 %all-to-all-start.5 = ((bf16[8,256,384]{1,2,0:T(8,128)(2,1)}), bf16[8,256,384]{1,2,0:T(8,128)(2,1)}, u32[]{:S(2)}, u32[]{:S(2)}) async-start(bf16[8,256,384]{1,2,0:T(8,128)(2,1)} %copy.136), calls=%async_computation.5 | async-start | bytes 3145728 | tf_op jit(solution)/shard_map/all_to_all | solution.py:121
  93.3 0.6 convert_bitcast_fusion
  93.8 5.5 %copy.119 = f32[16,2,12,3072]{3,2,1,0:T(8,128)} copy(f32[16,2,12,3072]{3,0,2,1:T(8,128)S(1)} %convert_bitcast_fusion) | data formatting | bytes 9437184 | tf_op jit(solution)/shard_map/convert_element_type | solution.py:54
  99.3 5.4 %reshape.105 = f32[384,3072]{1,0:T(8,128)} reshape(f32[16,2,12,3072]{3,2,1,0:T(8,128)} %copy.119) | data formatting | bytes 9437184 | tf_op jit(solution)/shard_map/convert_element_type | solution.py:54
  104.8 77.1 %all-gather.3.cloned.1.call-done = bf16[1,2048,3072]{2,1,0:T(8,128)(2,1)} async-done(((bf16[1,256,3072]{2,1,0:T(8,128)(2,1)}), bf16[1,2048,3072]{2,1,0:T(8,128)(2,1)}) %all-gather.3.cloned.1.call-update) | async-done | bytes 12582928 | tf_op jit(solution)/shard_map/all_gather | solution.py:116
  181.9 10.8 %fusion.22 = bf16[1,2048,384]{1,2,0:T(8,128)(2,1)S(1)} fusion(bf16[1,2048,3072]{2,1,0:T(8,128)(2,1)} %all-gather.3.cloned.1.call-done, f32[384,3072]{1,0:T(8,128)} %reshape.105, f32[384,3072]{1,0:T(8,128)} %copy.122), kind=kOutput, calls=%fused_computation.21 | convolution fusion | flops 4834983936 | bytes 23592960 | tf_op jit(solution)/shard_map/dot_general | solution.py:123
  192.7 5.6 %copy.123 = bf16[1,2048,384]{2,0,1:T(2,128)(2,1)} copy(bf16[1,2048,384]{1,2,0:T(8,128)(2,1)S(1)} %fusion.22) | data formatting | bytes 3145728 | tf_op jit(solution)/shard_map/reshape | solution.py:143
  198.3 0.5 broadcast.35
  198.9 34.3 %reduce = bf16[2048,384]{1,0:T(8,128)(2,1)S(1)} reduce(bf16[2048,1,384]{2,1,0:T(2,128)(2,1)} %bitcast.68, bf16[]{:T(256)} %broadcast.35), dimensions={1}, to_apply=%bitcast.50.reduce_sub_computation | reduce | bytes 3145730
  233.2 1.9 reshape.111
  235.0 0.0 all-to-all-done.5
  235.0 14.1 %convolution_convert_fusion = bf16[8,384,3072]{2,1,0:T(8,128)(2,1)} fusion(bf16[8,256,384]{1,2,0:T(8,128)(2,1)} %all-to-all-done.5, bf16[8,256,3072]{2,1,0:T(8,128)(2,1)} %bitcast.70), kind=kOutput, calls=%fused_computation.5 | convolution fusion | flops 4841275392 | bytes 33030144 | tf_op jit(solution)/shard_map/rlp,rle->rpe/dot_general | solution.py:134
  249.1 12.8 %convert_reduce_fusion = f32[384,3072]{1,0:T(8,128)} fusion(bf16[8,384,3072]{2,1,0:T(8,128)(2,1)} %convolution_convert_fusion), kind=kLoop, calls=%fused_computation.2 | loop fusion | flops 17694720 | bytes 23592960 | tf_op jit(solution)/shard_map/reduce_sum | solution.py:138
  261.9 5.5 %reshape_reshape.9 = f32[16,2,12,3072]{3,2,1,0:T(8,128)} reshape(f32[384,3072]{1,0:T(8,128)} %convert_reduce_fusion) | data formatting | bytes 9437184 | tf_op jit(solution)/shard_map/reshape;reshape | solution.py:33
  267.4 5.5 %copy.137 = f32[2,16,12,3072]{3,1,2,0:T(8,128)S(1)} copy(f32[2,16,12,3072]{3,2,0,1:T(8,128)} %bitcast.66) | data formatting | bytes 9437184 | tf_op jit(solution)/shard_map/transpose | solution.py:33
  272.9 8.6 %all_to_all.50 = f32[2,16,12,3072]{3,1,2,0:T(8,128)} all-to-all(f32[2,16,12,3072]{3,1,2,0:T(8,128)S(1)} %copy.137), channel_id=1, replica_groups=mesh['group_0'=8,'group_1'=2,'group_2'=2,'rep'=8] {'group_2'}, dimensions={0} | all-to-all | bytes 9437184 | tf_op jit(solution)/shard_map/all_to_all | solution.py:38
  281.6 6.9 %all-to-all-start.4 = ((bf16[8,2,49152]{2,1,0:T(2,128)(2,1)}), bf16[8,2,49152]{2,1,0:T(2,128)(2,1)}, u32[]{:S(2)}, u32[]{:S(2)}) async-start(bf16[8,2,49152]{2,1,0:T(2,128)(2,1)} %reshape.111), calls=%async_computation.4 | async-start | bytes 3145728 | tf_op jit(solution)/shard_map/all_to_all | solution.py:142
  288.5 2.9 reduce_sum.50
  291.4 3.0 copy.138
  294.4 14.6 %all-to-all-done.4 = bf16[8,2,49152]{2,1,0:T(2,128)(2,1)} async-done(((bf16[8,2,49152]{2,1,0:T(2,128)(2,1)}), bf16[8,2,49152]{2,1,0:T(2,128)(2,1)}, u32[]{:S(2)}, u32[]{:S(2)}) %all-to-all-start.4) | async-done | bytes 1572896 | tf_op jit(solution)/shard_map/all_to_all | solution.py:142
  309.0 6.4 %all-to-all-start.7 = ((f32[16,12,3072]{2,1,0:T(8,128)}), f32[16,12,3072]{2,1,0:T(8,128)}, u32[]{:S(2)}, u32[]{:S(2)}) async-start(f32[16,12,3072]{2,1,0:T(8,128)} %copy.138), calls=%async_computation.7 | async-start | bytes 6291456 | tf_op jit(solution)/shard_map/all_to_all | solution.py:46
  315.5 6.3 %reshape.112 = bf16[2048,1,384]{2,1,0:T(2,128)(2,1)} reshape(bf16[8,2,49152]{2,1,0:T(2,128)(2,1)} %all-to-all-done.4) | data formatting | bytes 3145728
  321.8 6.8 %copy.124 = bf16[1,2048,384]{1,2,0:T(8,128)(2,1)S(1)} copy(bf16[1,2048,384]{2,0,1:T(2,128)(2,1)} %bitcast.69) | data formatting | bytes 3145728 | tf_op jit(solution)/shard_map/all_to_all | solution.py:142
  328.6 0.5 copy.150
  329.1 0.5 copy.125
  329.6 1.3 reshape.101
  331.0 5.6 %convolution_convert_fusion.2 = bf16[24,128,256]{2,1,0:T(8,128)(2,1)} fusion(bf16[256,24,128]{0,2,1:T(8,128)(2,1)} %reshape.101, f32[24,256,256]{1,2,0:T(8,128)} %get-tuple-element.74, f32[24,256]{1,0:T(8,128)S(1)} %get-tuple-element.73), kind=kOutput, calls=%fused_computation.25 | convolution fusion | flops 406585344 | bytes 9461760 | tf_op jit(solution)/shard_map/while/body/eval_jaxpr/hqk,qhd->khd/dot_general | solution.py:88
  336.6 2.7 copy.141
  339.3 5.1 %fusion.44 = f32[24,256,256]{1,2,0:T(8,128)} fusion(bf16[256,24,128]{0,2,1:T(8,128)(2,1)} %bitcast.73, bf16[256,24,128]{0,2,1:T(8,128)(2,1)S(1)} %copy-done.2), kind=kOutput, calls=%fused_computation.40 | convolution fusion | flops 402653184 | bytes 9437184 | tf_op jit(solution)/shard_map/while/body/eval_jaxpr/qhd,khd->hqk/dot_general | solution.py:91
  344.3 12.2 %fusion.25 = bf16[24,256,128]{1,2,0:T(8,128)(2,1)} fusion(bf16[256,24,128]{0,2,1:T(8,128)(2,1)} %bitcast.80, f32[24,256,256]{1,2,0:T(8,128)} %fusion.44, f32[24,256,256]{1,2,0:T(8,128)} %get-tuple-element.74, f32[24,256]{1,0:T(8,128)S(1)} %get-tuple-element.73), kind=kOutput, calls=%fused_computation.22 | convolution fusion | flops 414456064 | bytes 15753216 | tf_op jit(solution)/shard_map/while/body/eval_jaxpr/hqk,khd->qhd/dot_general | solution.py:94
  356.5 2.7 copy.139
  359.2 11.9 %fusion.28 = bf16[24,256,128]{1,2,0:T(8,128)(2,1)} fusion(bf16[256,24,128]{0,2,1:T(8,128)(2,1)S(1)} %bitcast.78, f32[24,256,256]{1,2,0:T(8,128)} %fusion.44, f32[24,256,256]{1,2,0:T(8,128)} %get-tuple-element.74, f32[24,256]{1,0:T(8,128)S(1)} %get-tuple-element.73), kind=kOutput, calls=%fused_computation.23 | convolution fusion | flops 414456064 | bytes 15753216 | tf_op jit(solution)/shard_map/while/body/eval_jaxpr/hqk,qhd->khd/dot_general | solution.py:95
  371.1 2.6 copy.140
  373.8 15.1 %all-to-all-done.7 = f32[16,12,3072]{2,1,0:T(8,128)} async-done(((f32[16,12,3072]{2,1,0:T(8,128)}), f32[16,12,3072]{2,1,0:T(8,128)}, u32[]{:S(2)}, u32[]{:S(2)}) %all-to-all-start.7) | async-done | bytes 2359328 | tf_op jit(solution)/shard_map/all_to_all | solution.py:46
  388.8 2.8 reduce_sum.51
  (14 shorter events, 0.1 us)
Async XLA Ops:
  7.2 11.5 %copy-start = (bf16[96,3072]{1,0:T(8,128)(2,1)S(1)}, bf16[96,3072]{1,0:T(8,128)(2,1)}, u32[]{:S(2)}) copy-start(bf16[96,3072]{1,0:T(8,128)(2,1)} %param.10) | copy-start | bytes 1769476
  7.2 174.7 %all-gather.3.cloned.1.call-start = ((), (), s32[]{:S(2)}) async-start(), calls=%async_computation.8 | async-start | bytes 14155776 | tf_op jit(solution)/shard_map/all_gather | solution.py:116
  7.9 29.5 %copy-start.4 = (bf16[1,256,3072]{2,1,0:T(8,128)(2,1)S(1)}, bf16[1,256,3072]{2,1,0:T(8,128)(2,1)}, u32[]{:S(2)}) copy-start(bf16[1,256,3072]{2,1,0:T(8,128)(2,1)} %param.6) | copy-start | bytes 4718596
  9.5 18.3 %all-to-all-start.2 = ((bf16[16,12,12]{1,2,0:T(8,128)(2,1)}), bf16[16,12,12]{1,2,0:T(8,128)(2,1)S(1)}, u32[]{:S(2)}, u32[]{:S(2)}) async-start(bf16[16,12,12]{1,2,0:T(8,128)(2,1)} %broadcast_in_dim.52), calls=%async_computation.2 | async-start | bytes 131072 | tf_op jit(solution)/shard_map/all_to_all | solution.py:14
  33.0 44.4 %all-to-all-start = ((bf16[16,12,3072]{2,1,0:T(8,128)(2,1)}), bf16[16,12,3072]{2,1,0:T(8,128)(2,1)}, u32[]{:S(2)}, u32[]{:S(2)}) async-start(bf16[16,12,3072]{2,1,0:T(8,128)(2,1)} %broadcast_in_dim.50), calls=%async_computation | async-start | bytes 3145728 | tf_op jit(solution)/shard_map/all_to_all | solution.py:14
  43.3 7.4 %copy-start.3 = (bf16[1,256,3072]{1,2,0:T(8,128)(2,1)}, bf16[1,256,3072]{1,2,0:T(8,128)(2,1)S(1)}, u32[]{:S(2)}) copy-start(bf16[1,256,3072]{1,2,0:T(8,128)(2,1)S(1)} %copy.149) | copy-start | bytes 4718596
  85.3 149.7 %all-to-all-start.5 = ((bf16[8,256,384]{1,2,0:T(8,128)(2,1)}), bf16[8,256,384]{1,2,0:T(8,128)(2,1)}, u32[]{:S(2)}, u32[]{:S(2)}) async-start(bf16[8,256,384]{1,2,0:T(8,128)(2,1)} %copy.136), calls=%async_computation.5 | async-start | bytes 3145728 | tf_op jit(solution)/shard_map/all_to_all | solution.py:121
  281.6 27.5 %all-to-all-start.4 = ((bf16[8,2,49152]{2,1,0:T(2,128)(2,1)}), bf16[8,2,49152]{2,1,0:T(2,128)(2,1)}, u32[]{:S(2)}, u32[]{:S(2)}) async-start(bf16[8,2,49152]{2,1,0:T(2,128)(2,1)} %reshape.111), calls=%async_computation.4 | async-start | bytes 3145728 | tf_op jit(solution)/shard_map/all_to_all | solution.py:142
  309.0 79.8 %all-to-all-start.7 = ((f32[16,12,3072]{2,1,0:T(8,128)}), f32[16,12,3072]{2,1,0:T(8,128)}, u32[]{:S(2)}, u32[]{:S(2)}) async-start(f32[16,12,3072]{2,1,0:T(8,128)} %copy.138), calls=%async_computation.7 | async-start | bytes 6291456 | tf_op jit(solution)/shard_map/all_to_all | solution.py:46
  336.6 2.7 copy-start.2
  356.5 2.7 copy-start.5
  371.1 20.5 %copy-start.1 = (bf16[96,3072]{1,0:T(8,128)(2,1)S(1)}, bf16[96,3072]{1,0:T(8,128)(2,1)}, u32[]{:S(2)}) copy-start(bf16[96,3072]{1,0:T(8,128)(2,1)} %param.10) | copy-start | bytes 1769476
Sparse Core Ops, SparseCore 0:
  10.6 171.2 all-gather.2
where the time goes:
time: 406 us; the launch traced here: 399 us
  waiting for transfers between devices  125 us (31%)
  local copies, waits for them, and re-layouts  81.5 us (20%)
  matrix products  71.7 us (18%)
  other arithmetic  53.3 us (13%)
  starting transfers between devices  35 us (9%)
  blocking collectives  18 us (4%)
  between operations  14.5 us (4%)
    all_gather x1, waiting for transfers between devices, per_device(): all_output = lax.all_gather(output_flat, 'rep', axis=0, tiled=True)  77.1 us
    unnamed x1, other arithmetic  34.3 us
    unnamed x22, local copies, waits for them, and re-layouts  17.7 us
    all_to_all x2, waiting for transfers between devices, from_everyone(): lax.all_to_all(jnp.broadcast_to(value[None], (count, *value.shape)), axis...  17.3 us
    all_to_all x1, waiting for transfers between devices, sum_in_two_steps(): lax.all_to_all(nearer, far, split_axis=0, concat_axis=0, tiled=True)  15.1 us
    all_to_all x1, waiting for transfers between devices, per_device(): lax.all_to_all(grad_columns.reshape(1, replica_count * local_rows, group_...  14.6 us
    dot_general x1, matrix products, per_device(): jnp.einsum('rlp,rle->rpe', gathered_ctx, output_blocks, preferred_element...  14.1 us
    all_to_all x2, starting transfers between devices, from_everyone(): lax.all_to_all(jnp.broadcast_to(value[None], (count, *value.shape)), axis...  13.6 us
  transfers between devices with their start and end apart: 6, of which 5 were waited for; matrix products, arithmetic and copies ran while one was open for 42% of the time, Pallas kernels for 0%

commit v1 on v0

--- a/solution.py
+++ b/solution.py
@@ -113,7 +113,9 @@
     first_row = lax.axis_index("rep") * slab_rows
     codes_part = lax.dynamic_slice_in_dim(weight_codes, first_row, slab_rows, 0)
     scales_part = lax.dynamic_slice_in_dim(weight_scales, first_row, slab_rows, 0)
-    all_output = lax.all_gather(output_flat, "rep", axis=0, tiled=True)
+    all_output = jnp.concatenate(
+        lax.all_to_all(jnp.stack([output_flat] * lax.axis_size("rep")), "rep", 0, 0), axis=0
+    )
     split_context = jnp.moveaxis(
         context_flat.reshape(local_rows, group_count, replica_count, slab_rows), 2, 0
     )

time: 406 us -> 461 us (1.14)
  waiting for transfers between devices: 125 us -> 174 us
  local copies, waits for them, and re-layouts: 81.5 us -> 96.3 us
  between operations: 14.5 us -> 1.05 us
  starting transfers between devices: 35 us -> 42 us
  other arithmetic: 53.3 us -> 59 us
    all_to_all x0 -> x1, waiting for transfers between devices: none -> 96.7 us  [per_device(): lax.all_to_all(jnp.stack([output_flat] * lax.axis_size('rep')), 'rep', 0, 0)]
    all_gather x1 -> x0, waiting for transfers between devices: 77.1 us -> none  [per_device(): all_output = lax.all_gather(output_flat, 'rep', axis=0, tiled=True)]
    all_to_all x2 -> x3, waiting for transfers between devices: 17.3 us -> 47.4 us  [from_everyone(): lax.all_to_all(jnp.broadcast_to(value[None], (count, *value.shape)), axis...]
    mul x2 -> x0, local copies, waits for them, and re-layouts: 8.51 us -> none  [restore(): code_rows.astype(jnp.float32).reshape(row_count, block_count, -1)]
    all_to_all x0 -> x1, starting transfers between devices: none -> 7.78 us  [per_device(): lax.all_to_all(jnp.stack([output_flat] * lax.axis_size('rep')), 'rep', 0, 0)]
    another operation x0 -> x1, local copies, waits for them, and re-layouts: none -> 7.58 us  [per_device(): jnp.stack([output_flat] * lax.axis_size('rep'))]
    convert_element_type x0 -> x1, local copies, waits for them, and re-layouts: none -> 4.84 us  [restore(): return spread.reshape(row_count, -1).astype(jnp.bfloat16)]
    all_to_all x2 -> x1, blocking collectives: 9.34 us -> 5.63 us  [from_everyone(): lax.all_to_all(jnp.broadcast_to(value[None], (count, *value.shape)), axis...]
  transfers between devices with their start and end apart: 6 -> 7, of which waited for: 5 -> 6; matrix products, arithmetic and copies ran while one was open for 42% -> 38% of each run, Pallas kernels for 0% -> 0%
where the time goes in v1:
time: 461 us; the launch traced here: 456 us
  waiting for transfers between devices  174 us (38%)
  local copies, waits for them, and re-layouts  96.3 us (21%)
  matrix products  69.7 us (15%)
  other arithmetic  59 us (13%)
  starting transfers between devices  42 us (9%)
  blocking collectives  14.2 us (3%)
    all_to_all x1, waiting for transfers between devices, per_device(): lax.all_to_all(jnp.stack([output_flat] * lax.axis_size('rep')), 'rep', 0, 0)  96.7 us
    all_to_all x3, waiting for transfers between devices, from_everyone(): lax.all_to_all(jnp.broadcast_to(value[None], (count, *value.shape)), axis...  47.4 us
    unnamed x1, other arithmetic  35.5 us
    unnamed x20, local copies, waits for them, and re-layouts  20.1 us
    all_to_all x3, starting transfers between devices, from_everyone(): lax.all_to_all(jnp.broadcast_to(value[None], (count, *value.shape)), axis...  16.1 us
    all_to_all x1, waiting for transfers between devices, sum_in_two_steps(): lax.all_to_all(nearer, far, split_axis=0, concat_axis=0, tiled=True)  15.7 us
    all_to_all x1, waiting for transfers between devices, per_device(): lax.all_to_all(grad_columns.reshape(1, replica_count * local_rows, group_...  14.3 us
    dot_general x1, matrix products, per_device(): jnp.einsum('rlp,rle->rpe', gathered_ctx, output_blocks, preferred_element...  13.8 us
  transfers between devices with their start and end apart: 7, of which 6 were waited for; matrix products, arithmetic and copies ran while one was open for 38% of the time, Pallas kernels for 0%

profile of v1, /device:TPU:4, one launch (start us, length us, event | category | flops | bytes accessed | tf_op | source)
XLA Modules:
  0.0 456.4 jit_solution(2358437438961326919)
XLA Ops:
  0.6 0.0 copy-start
  0.7 0.8 dynamic-slice_convert_fusion
  1.5 0.6 broadcast_in_dim.52
  2.1 9.2 %all-to-all-start.2 = ((bf16[16,12,12]{1,2,0:T(8,128)(2,1)}), bf16[16,12,12]{1,2,0:T(8,128)(2,1)S(1)}, u32[]{:S(2)}, u32[]{:S(2)}) async-start(bf16[16,12,12]{1,2,0:T(8,128)(2,1)} %broadcast_in_dim.52), calls=%async_computation.2 | async-start | bytes 131072 | tf_op jit(solution)/shard_map/all_to_all | solution.py:14
  11.3 0.0 copy-done
  11.4 9.0 %all-to-all-done.2 = bf16[16,12,12]{1,2,0:T(8,128)(2,1)S(1)} async-done(((bf16[16,12,12]{1,2,0:T(8,128)(2,1)}), bf16[16,12,12]{1,2,0:T(8,128)(2,1)S(1)}, u32[]{:S(2)}, u32[]{:S(2)}) %all-to-all-start.2) | async-done | bytes 4640 | tf_op jit(solution)/shard_map/all_to_all | solution.py:14
  20.4 1.3 broadcast_in_dim.50
  21.7 3.7 all-to-all-start
  25.5 0.8 reshape.119
  26.2 37.7 %all-to-all-done = bf16[16,12,3072]{2,1,0:T(8,128)(2,1)S(1)} async-done(((bf16[16,12,3072]{2,1,0:T(8,128)(2,1)}), bf16[16,12,3072]{2,1,0:T(8,128)(2,1)S(1)}, u32[]{:S(2)}, u32[]{:S(2)}) %all-to-all-start) | async-done | bytes 1179680 | tf_op jit(solution)/shard_map/all_to_all | solution.py:14
  63.9 3.2 all-to-all-start.3
  67.2 0.7 copy.122
  67.8 0.7 all-to-all-done.3
  68.5 0.3 broadcast_in_dim.51
  68.8 5.6 %all_to_all.53 = bf16[2,16,12,3072]{3,1,2,0:T(8,128)(2,1)S(1)} all-to-all(bf16[2,16,12,3072]{3,1,2,0:T(8,128)(2,1)S(1)} %broadcast_in_dim.51), channel_id=1, replica_groups=mesh['group_0'=8,'group_1'=2,'group_2'=2,'rep'=8] {'group_2'}, dimensions={0} | all-to-all | bytes 4718592 | tf_op jit(solution)/shard_map/all_to_all | solution.py:14
  74.4 7.6 %stack.3 = bf16[8,256,3072]{2,1,0:T(8,128)(2,1)} broadcast(bf16[256,3072]{1,0:T(8,128)(2,1)} %bitcast.70), dimensions={1,2} | broadcast | bytes 14155776 | tf_op jit(solution)/shard_map/stack | solution.py:117
  82.0 7.8 %all-to-all-start.4 = ((bf16[8,256,3072]{2,1,0:T(8,128)(2,1)}), bf16[8,256,3072]{2,1,0:T(8,128)(2,1)}, u32[]{:S(2)}, u32[]{:S(2)}) async-start(bf16[8,256,3072]{2,1,0:T(8,128)(2,1)} %stack.3), calls=%async_computation.4 | async-start | bytes 25165824 | tf_op jit(solution)/shard_map/all_to_all | solution.py:117
  89.8 2.6 copy.156
  92.4 2.6 copy.154
  94.9 2.6 copy.155
  97.5 6.8 %fusion.36 = (f32[24,256]{1,0:T(8,128)S(1)}, f32[24,256,256]{1,2,0:T(8,128)}) fusion(bf16[256,24,128]{0,2,1:T(8,128)(2,1)} %bitcast.73, bf16[256,24,128]{0,2,1:T(8,128)(2,1)} %bitcast.71), kind=kOutput, calls=%fused_computation.36 | convolution fusion | flops 407372032 | bytes 9461760 | tf_op jit(solution)/shard_map/while/body/eval_jaxpr/sub | solution.py:70
  104.3 5.1 %fusion.26 = bf16[256,24,128]{0,2,1:T(8,128)(2,1)} fusion(bf16[256,24,128]{0,2,1:T(8,128)(2,1)} %bitcast.64, f32[24,256,256]{1,2,0:T(8,128)} %get-tuple-element.74, f32[24,256]{1,0:T(8,128)S(1)} %get-tuple-element.73), kind=kOutput, calls=%fused_computation.26 | convolution fusion | flops 406585344 | bytes 9461760 | tf_op jit(solution)/shard_map/while/body/eval_jaxpr/hqk,khd->qhd/dot_general | solution.py:73
  109.4 3.7 reshape_reshape.8
  113.1 2.3 copy.140
  115.4 1.5 copy.141
  116.9 0.2 reshape.120
  117.1 0.3 copy.152
  117.5 0.6 convert_bitcast_fusion
  118.0 5.5 %copy.123 = f32[16,2,12,3072]{3,2,1,0:T(8,128)} copy(f32[16,2,12,3072]{3,0,2,1:T(8,128)S(1)} %convert_bitcast_fusion) | data formatting | bytes 9437184 | tf_op jit(solution)/shard_map/convert_element_type | solution.py:54
  123.5 7.8 %reshape.116 = f32[384,12,256]{2,1,0:T(8,128)} reshape(f32[16,2,12,3072]{3,2,1,0:T(8,128)} %copy.123) | data formatting | bytes 9437184 | tf_op jit(solution)/shard_map/convert_element_type | solution.py:54
  131.3 96.7 %all-to-all-done.4 = bf16[8,256,3072]{2,1,0:T(8,128)(2,1)} async-done(((bf16[8,256,3072]{2,1,0:T(8,128)(2,1)}), bf16[8,256,3072]{2,1,0:T(8,128)(2,1)}, u32[]{:S(2)}, u32[]{:S(2)}) %all-to-all-start.4) | async-done | bytes 12582944 | tf_op jit(solution)/shard_map/all_to_all | solution.py:117
  228.0 6.2 %all-to-all-start.6 = ((bf16[8,256,384]{1,2,0:T(8,128)(2,1)}), bf16[8,256,384]{1,2,0:T(8,128)(2,1)S(1)}, u32[]{:S(2)}, u32[]{:S(2)}) async-start(bf16[8,256,384]{1,2,0:T(8,128)(2,1)} %copy.141), calls=%async_computation.6 | async-start | bytes 3145728 | tf_op jit(solution)/shard_map/all_to_all | solution.py:123
  234.2 4.5 multiply_convert_fusion.1
  238.7 4.8 %copy.127 = bf16[384,12,256]{0,2,1:T(8,128)(2,1)} copy(bf16[384,12,256]{2,1,0:T(8,128)(2,1)} %multiply_convert_fusion.1) | data formatting | bytes 4718592 | tf_op jit(solution)/shard_map/convert_element_type | solution.py:56
  243.5 9.7 %fusion.17 = bf16[1,2048,384]{1,2,0:T(8,128)(2,1)} fusion(bf16[384,3072]{0,1:T(8,128)(2,1)} %bitcast.69, bf16[2048,3072]{1,0:T(8,128)(2,1)} %bitcast.4), kind=kOutput, calls=%fused_computation.19 | convolution fusion | flops 4832624640 | bytes 16515072 | tf_op jit(solution)/shard_map/dot_general | solution.py:125
  253.2 8.4 %copy.128 = bf16[1,2048,384]{2,0,1:T(2,128)(2,1)} copy(bf16[1,2048,384]{1,2,0:T(8,128)(2,1)} %fusion.17) | data formatting | bytes 3145728 | tf_op jit(solution)/shard_map/reshape | solution.py:145
  261.7 0.5 broadcast.39
  262.2 35.5 %reduce = bf16[2048,384]{1,0:T(8,128)(2,1)} reduce(bf16[2048,1,384]{2,1,0:T(2,128)(2,1)} %bitcast.61, bf16[]{:T(256)} %broadcast.39), dimensions={1}, to_apply=%bitcast.42.reduce_sub_computation | reduce | bytes 3145730
  297.6 3.7 reshape.121
  301.4 0.0 all-to-all-done.6
  301.4 13.8 %convolution_convert_fusion = bf16[8,384,3072]{2,1,0:T(8,128)(2,1)} fusion(bf16[8,256,384]{1,2,0:T(8,128)(2,1)S(1)} %all-to-all-done.6, bf16[8,256,3072]{2,1,0:T(8,128)(2,1)} %all-to-all-done.4), kind=kOutput, calls=%fused_computation.3 | convolution fusion | flops 4841275392 | bytes 33030144 | tf_op jit(solution)/shard_map/rlp,rle->rpe/dot_general | solution.py:136
  315.2 12.8 %convert_reduce_fusion = f32[384,3072]{1,0:T(8,128)} fusion(bf16[8,384,3072]{2,1,0:T(8,128)(2,1)} %convolution_convert_fusion), kind=kLoop, calls=%fused_computation.2 | loop fusion | flops 17694720 | bytes 23592960 | tf_op jit(solution)/shard_map/reduce_sum | solution.py:140
  328.0 5.5 %reshape_reshape.9 = f32[16,2,12,3072]{3,2,1,0:T(8,128)} reshape(f32[384,3072]{1,0:T(8,128)} %convert_reduce_fusion) | data formatting | bytes 9437184 | tf_op jit(solution)/shard_map/reshape;reshape | solution.py:33
  333.5 5.5 %copy.142 = f32[2,16,12,3072]{3,1,2,0:T(8,128)S(1)} copy(f32[2,16,12,3072]{3,2,0,1:T(8,128)} %bitcast.60) | data formatting | bytes 9437184 | tf_op jit(solution)/shard_map/transpose | solution.py:33
  339.0 8.6 %all_to_all.54 = f32[2,16,12,3072]{3,1,2,0:T(8,128)} all-to-all(f32[2,16,12,3072]{3,1,2,0:T(8,128)S(1)} %copy.142), channel_id=1, replica_groups=mesh['group_0'=8,'group_1'=2,'group_2'=2,'rep'=8] {'group_2'}, dimensions={0} | all-to-all | bytes 9437184 | tf_op jit(solution)/shard_map/all_to_all | solution.py:38
  347.6 7.2 %all-to-all-start.5 = ((bf16[8,2,49152]{2,1,0:T(2,128)(2,1)}), bf16[8,2,49152]{2,1,0:T(2,128)(2,1)}, u32[]{:S(2)}, u32[]{:S(2)}) async-start(bf16[8,2,49152]{2,1,0:T(2,128)(2,1)} %reshape.121), calls=%async_computation.5 | async-start | bytes 3145728 | tf_op jit(solution)/shard_map/all_to_all | solution.py:144
  354.8 2.9 reduce_sum.50
  357.8 3.1 copy.143
  360.8 14.3 %all-to-all-done.5 = bf16[8,2,49152]{2,1,0:T(2,128)(2,1)} async-done(((bf16[8,2,49152]{2,1,0:T(2,128)(2,1)}), bf16[8,2,49152]{2,1,0:T(2,128)(2,1)}, u32[]{:S(2)}, u32[]{:S(2)}) %all-to-all-start.5) | async-done | bytes 1572896 | tf_op jit(solution)/shard_map/all_to_all | solution.py:144
  375.1 4.7 %all-to-all-start.8 = ((f32[16,12,3072]{2,1,0:T(8,128)}), f32[16,12,3072]{2,1,0:T(8,128)}, u32[]{:S(2)}, u32[]{:S(2)}) async-start(f32[16,12,3072]{2,1,0:T(8,128)} %copy.143), calls=%async_computation.8 | async-start | bytes 6291456 | tf_op jit(solution)/shard_map/all_to_all | solution.py:46
  379.8 6.3 %reshape.122 = bf16[2048,1,384]{2,1,0:T(2,128)(2,1)} reshape(bf16[8,2,49152]{2,1,0:T(2,128)(2,1)} %all-to-all-done.5) | data formatting | bytes 3145728
  386.2 6.8 %copy.129 = bf16[1,2048,384]{1,2,0:T(8,128)(2,1)S(1)} copy(bf16[1,2048,384]{2,0,1:T(2,128)(2,1)} %bitcast.62) | data formatting | bytes 3145728 | tf_op jit(solution)/shard_map/all_to_all | solution.py:144
  392.9 0.5 copy.157
  393.4 0.5 copy.130
  393.9 1.3 reshape.113
  395.3 5.7 %fusion.37 = f32[24,256,256]{1,2,0:T(8,128)} fusion(bf16[256,24,128]{0,2,1:T(8,128)(2,1)} %bitcast.65, bf16[256,24,128]{0,2,1:T(8,128)(2,1)} %reshape.113), kind=kOutput, calls=%fused_computation.38 | convolution fusion | flops 402653184 | bytes 9437184 | tf_op jit(solution)/shard_map/while/body/eval_jaxpr/qhd,khd->hqk/dot_general | solution.py:91
  401.0 11.8 %fusion.21 = bf16[24,256,128]{1,2,0:T(8,128)(2,1)} fusion(bf16[256,24,128]{0,2,1:T(8,128)(2,1)S(1)} %bitcast.74, f32[24,256,256]{1,2,0:T(8,128)} %fusion.37, f32[24,256,256]{1,2,0:T(8,128)} %get-tuple-element.74, f32[24,256]{1,0:T(8,128)S(1)} %get-tuple-element.73), kind=kOutput, calls=%fused_computation.21 | convolution fusion | flops 414456064 | bytes 15753216 | tf_op jit(solution)/shard_map/while/body/eval_jaxpr/hqk,qhd->khd/dot_general | solution.py:95
  412.8 2.7 copy.145
  415.5 11.7 %fusion.18 = bf16[24,256,128]{1,2,0:T(8,128)(2,1)} fusion(bf16[256,24,128]{0,2,1:T(8,128)(2,1)S(1)} %bitcast.72, f32[24,256,256]{1,2,0:T(8,128)} %fusion.37, f32[24,256,256]{1,2,0:T(8,128)} %get-tuple-element.74, f32[24,256]{1,0:T(8,128)S(1)} %get-tuple-element.73), kind=kOutput, calls=%fused_computation.20 | convolution fusion | flops 414456064 | bytes 15753216 | tf_op jit(solution)/shard_map/while/body/eval_jaxpr/hqk,khd->qhd/dot_general | solution.py:94
  427.2 2.7 copy.144
  429.9 5.1 %convolution_convert_fusion.3 = bf16[24,128,256]{2,1,0:T(8,128)(2,1)} fusion(bf16[256,24,128]{0,2,1:T(8,128)(2,1)S(1)} %copy-done.2, f32[24,256,256]{1,2,0:T(8,128)} %get-tuple-element.74, f32[24,256]{1,0:T(8,128)S(1)} %get-tuple-element.73), kind=kOutput, calls=%fused_computation.23 | convolution fusion | flops 406585344 | bytes 9461760 | tf_op jit(solution)/shard_map/while/body/eval_jaxpr/hqk,qhd->khd/dot_general | solution.py:88
  435.0 2.6 copy.146
  437.7 15.7 %all-to-all-done.8 = f32[16,12,3072]{2,1,0:T(8,128)} async-done(((f32[16,12,3072]{2,1,0:T(8,128)}), f32[16,12,3072]{2,1,0:T(8,128)}, u32[]{:S(2)}, u32[]{:S(2)}) %all-to-all-start.8) | async-done | bytes 2359328 | tf_op jit(solution)/shard_map/all_to_all | solution.py:46
  453.4 2.8 reduce_sum.51
  (13 shorter events, 0.1 us)
Async XLA Ops:
  0.6 10.7 %copy-start = (bf16[96,3072]{1,0:T(8,128)(2,1)S(1)}, bf16[96,3072]{1,0:T(8,128)(2,1)}, u32[]{:S(2)}) copy-start(bf16[96,3072]{1,0:T(8,128)(2,1)} %param.10) | copy-start | bytes 1769476
  2.1 18.3 %all-to-all-start.2 = ((bf16[16,12,12]{1,2,0:T(8,128)(2,1)}), bf16[16,12,12]{1,2,0:T(8,128)(2,1)S(1)}, u32[]{:S(2)}, u32[]{:S(2)}) async-start(bf16[16,12,12]{1,2,0:T(8,128)(2,1)} %broadcast_in_dim.52), calls=%async_computation.2 | async-start | bytes 131072 | tf_op jit(solution)/shard_map/all_to_all | solution.py:14
  21.7 42.2 %all-to-all-start = ((bf16[16,12,3072]{2,1,0:T(8,128)(2,1)}), bf16[16,12,3072]{2,1,0:T(8,128)(2,1)S(1)}, u32[]{:S(2)}, u32[]{:S(2)}) async-start(bf16[16,12,3072]{2,1,0:T(8,128)(2,1)} %broadcast_in_dim.50), calls=%async_computation | async-start | bytes 3145728 | tf_op jit(solution)/shard_map/all_to_all | solution.py:14
  63.9 4.6 %all-to-all-start.3 = ((bf16[2,2,1152]{2,1,0:T(2,128)(2,1)}), bf16[2,2,1152]{2,1,0:T(2,128)(2,1)S(1)}, u32[]{:S(2)}, u32[]{:S(2)}) async-start(bf16[2,2,1152]{2,1,0:T(2,128)(2,1)} %reshape.119), calls=%async_computation.3 | async-start | bytes 18432 | tf_op jit(solution)/shard_map/all_to_all | solution.py:14
  82.0 146.0 %all-to-all-start.4 = ((bf16[8,256,3072]{2,1,0:T(8,128)(2,1)}), bf16[8,256,3072]{2,1,0:T(8,128)(2,1)}, u32[]{:S(2)}, u32[]{:S(2)}) async-start(bf16[8,256,3072]{2,1,0:T(8,128)(2,1)} %stack.3), calls=%async_computation.4 | async-start | bytes 25165824 | tf_op jit(solution)/shard_map/all_to_all | solution.py:117
  228.0 73.4 %all-to-all-start.6 = ((bf16[8,256,384]{1,2,0:T(8,128)(2,1)}), bf16[8,256,384]{1,2,0:T(8,128)(2,1)S(1)}, u32[]{:S(2)}, u32[]{:S(2)}) async-start(bf16[8,256,384]{1,2,0:T(8,128)(2,1)} %copy.141), calls=%async_computation.6 | async-start | bytes 3145728 | tf_op jit(solution)/shard_map/all_to_all | solution.py:123
  347.6 27.5 %all-to-all-start.5 = ((bf16[8,2,49152]{2,1,0:T(2,128)(2,1)}), bf16[8,2,49152]{2,1,0:T(2,128)(2,1)}, u32[]{:S(2)}, u32[]{:S(2)}) async-start(bf16[8,2,49152]{2,1,0:T(2,128)(2,1)} %reshape.121), calls=%async_computation.5 | async-start | bytes 3145728 | tf_op jit(solution)/shard_map/all_to_all | solution.py:144
  375.1 78.3 %all-to-all-start.8 = ((f32[16,12,3072]{2,1,0:T(8,128)}), f32[16,12,3072]{2,1,0:T(8,128)}, u32[]{:S(2)}, u32[]{:S(2)}) async-start(f32[16,12,3072]{2,1,0:T(8,128)} %copy.143), calls=%async_computation.8 | async-start | bytes 6291456 | tf_op jit(solution)/shard_map/all_to_all | solution.py:46
  395.3 5.7 %copy-start.4 = (bf16[1,256,3072]{1,2,0:T(8,128)(2,1)S(1)}, bf16[1,256,3072]{1,2,0:T(8,128)(2,1)}, u32[]{:S(2)}) copy-start(bf16[1,256,3072]{1,2,0:T(8,128)(2,1)} %copy.155) | copy-start | bytes 4718596
  412.8 2.7 copy-start.3
  427.2 2.7 copy-start.2
  435.0 21.1 %copy-start.1 = (bf16[96,3072]{1,0:T(8,128)(2,1)S(1)}, bf16[96,3072]{1,0:T(8,128)(2,1)}, u32[]{:S(2)}) copy-start(bf16[96,3072]{1,0:T(8,128)(2,1)} %param.10) | copy-start | bytes 1769476
